TPU v7x, 32 devices: a whole 2x2x4 slice. The times are simulated.
32 devices in a mesh: depth: 4 (over z), tile: 8 (over y, x, core).
Axes of the slice: x: 2, y: 2, z: 4, core: 2. Of those that a mesh axis runs over, the one named last changes fastest.
Arguments:
- patches: float32 [512, 64, 1024], P('tile', 'depth'), may hold values from 0.1 to 10
- patch_slot: int32 [512], P('tile'), may hold values from 0 to 511, as said below
Outputs:
- image: float32 [8, 64, 4, 1024], P('tile', 'depth')
Inputs may be any that keep to these rules, and one draw needn't show every extreme that they name: patch_slot is a permutation of the slots. Device s of tile (patches s * 64 to (s + 1) * 64 - 1) sends to owner t a number that depends only on (t - s) mod 8: one such difference, drawn from the seed, carries 24 patches, two carry none, the others 64 // 8. Every owner receives 64 patches.
All inputs are finite; a program needn't handle non-finite values.
Results may differ from a plain program's by a relative error of at most 0.00002.
Values sent between devices are 32-bit elements; how exact they have to be, the bound alone decides.
A program may use at most 128 MiB of HBM per device.

v0:
```python
import jax
import jax.numpy as jnp
from jax import lax
from jax.sharding import PartitionSpec as P


def extended(block, sides, width):
    for axis, dim in sides:
        count = lax.axis_size(axis)
        forward = [(i, i + 1) for i in range(count - 1)]
        backward = [(target, source) for source, target in forward]
        low = lax.ppermute(
            lax.slice_in_dim(block, block.shape[dim] - width, None, axis=dim), axis, forward
        )
        high = lax.ppermute(lax.slice_in_dim(block, 0, width, axis=dim), axis, backward)
        block = jnp.concatenate([low, block, high], axis=dim)
    return block


def shade_rays(padded, depth_total):
    level = padded[:, 1:-1]
    slope = (padded[:, 2:] - padded[:, :-2]) * 0.5
    sigma = (
        0.6 * jnp.exp(-((level - 0.5) ** 2))
        + 0.4 * jnp.exp(-2.0 * (level + 1.0) ** 2)
        + 0.3 * slope * slope
    )
    optical = sigma * (2.0 / depth_total)
    depth_sum = jnp.cumsum(optical, axis=1)
    weight = jnp.exp(-(depth_sum - optical)) * (1.0 - jnp.exp(-optical))
    lighting = weight / (1.0 + slope * slope)
    red = jnp.sum(lighting * jax.nn.sigmoid(2.0 * level), axis=1)
    green = jnp.sum(lighting * jnp.exp(-level * level), axis=1)
    blue = jnp.sum(lighting * jax.nn.sigmoid(-2.0 * level), axis=1)
    remain = jnp.exp(-depth_sum[:, -1])
    return jnp.stack([red, green, blue, remain], axis=1)


def slab_layers(density):
    level = jnp.log(density)
    padded = extended(level, (("depth", 1),), 1)
    return shade_rays(padded, density.shape[1] * lax.axis_size("depth"))


def ranks_within(owners, groups):
    onehot = (owners[:, None] == jnp.arange(groups, dtype=jnp.int32)[None, :]).astype(jnp.int32)
    earlier = jnp.cumsum(onehot, axis=0) - onehot
    return jnp.sum(earlier * onehot, axis=1)


def pack_groups(values, dest, labels, groups, slots):
    target = dest * slots + ranks_within(dest, groups)
    buffer = jnp.zeros((groups * slots,) + values.shape[1:], jnp.float32).at[target].set(values)
    marks = (
        jnp.full((groups * slots,), -1.0, jnp.float32).at[target].set(labels.astype(jnp.float32))
    )
    return (buffer.reshape((groups, slots) + values.shape[1:]), marks.reshape(groups, slots))


def pack(values, patch_slot, tiles, slots):
    per = values.shape[0]
    return pack_groups(values, patch_slot // per, patch_slot % per, tiles, slots)


def place(received, labels, count):
    flat = received.reshape((-1,) + received.shape[2:])
    marks = labels.reshape(-1)
    target = jnp.where(marks >= 0.0, marks.astype(jnp.int32), count)
    return jnp.zeros((count + 1,) + flat.shape[1:], jnp.float32).at[target].set(flat)[:count]


def over(front, back):
    color = front[:, :3] + front[:, 3:] * back[:, :3]
    remain = front[:, 3:] * back[:, 3:]
    return jnp.concatenate([color, remain], axis=1)


def merge_depth(layers):
    depths = lax.axis_size("depth")
    pieces = lax.all_to_all(
        layers.reshape((1,) + layers.shape), "depth", split_axis=1, concat_axis=0, tiled=True
    )
    total = pieces[0]
    for level in range(1, depths):
        total = over(total, pieces[level])
    return total


def local(patches, patch_slot):
    per = patches.shape[0]
    tiles = lax.axis_size("tile")
    slots = 3 * per // tiles
    buffer, marks = pack(slab_layers(patches), patch_slot, tiles, slots)
    received, labels = (
        lax.all_to_all(buffer, "tile", split_axis=0, concat_axis=0, tiled=True),
        lax.all_to_all(marks, "tile", split_axis=0, concat_axis=0, tiled=True),
    )
    total = merge_depth(place(received, labels, per))
    color = total[:, :3]
    alpha = 1.0 - total[:, 3:]
    result = jnp.concatenate([color, alpha], axis=1)
    return result.reshape((1,) + result.shape)


def solution(mesh):
    return jax.shard_map(
        local,
        mesh=mesh,
        in_specs=(P("tile", "depth", None), P("tile")),
        out_specs=P("tile", "depth", None, None),
        check_vma=False,
    )
```

profile of v0, /device:TPU:0, one launch (start us, length us, event | category | flops | bytes accessed | tf_op | source)
XLA Modules:
  0.0 139.0 jit_solution(14399822710419634075)
XLA Ops:
  0.0 0.0 copy-start.2
  0.0 4.9 %copy_log_fusion = f32[64,16,1024]{2,0,1:T(8,128)S(1)} fusion(f32[64,16,1024]{2,1,0:T(8,128)} %param.2), kind=kLoop, calls=%fused_computation.10 | loop fusion | bytes 8388608 | tf_op jit(solution)/shard_map/log | solution.py:40
  4.9 0.0 copy-start.1
  4.9 1.9 %copy-done.1 = f32[64,16,1024]{2,0,1:T(8,128)} copy-done((f32[64,16,1024]{2,0,1:T(8,128)}, f32[64,16,1024]{2,0,1:T(8,128)S(1)}, u32[]{:S(2)}) %copy-start.1) | copy-done | bytes 4194328
  6.9 1.3 collective-permute-start
  8.2 5.6 %collective-permute-start.1 = (f32[64,1,1024]{2,0,1:T(8,128)S(1)}, f32[64,1,1024]{2,0,1:T(8,128)S(1)}, u32[]{:S(2)}, u32[]{:S(2)}) collective-permute-start(f32[64,1,1024]{2,0,1:T(8,128)S(1)} %get-tuple-element.12), channel_id=1, source_target_pairs={{0,8},{8,16},{16,24},{1,9},{9,17},{17,25},{2,10},{10,18},{18,26},{... | collective-permute-start | bytes 786440 | tf_op jit(solution)/shard_map/ppermute | solution.py:12
  13.8 0.0 copy-done.2
  13.8 0.1 fusion.10
  13.9 0.1 reduce_window_sum.22
  14.0 0.2 select_reduce_fusion
  14.2 0.8 scatter_custom_fusion
  15.0 0.7 all_to_all.18
  15.6 4.2 %all-to-all-start = ((f32[8,1,24]{2,1,0:T(1,128)}), f32[8,1,24]{2,1,0:T(1,128)S(1)}, u32[]{:S(2)}, u32[]{:S(2)}) async-start(f32[8,1,24]{2,1,0:T(1,128)} %all_to_all.18), calls=%async_computation | async-start | bytes 8192 | tf_op jit(solution)/shard_map/all_to_all | solution.py:96
  19.8 0.0 collective-permute-done
  19.8 0.0 collective-permute-done.1
  19.8 16.7 %multiply_reduce_fusion.1 = (f32[64,1024]{1,0:T(8,128)S(1)}, f32[64,1024]{1,0:T(8,128)S(1)}, f32[64,1024]{1,0:T(8,128)S(1)}, f32[64,16,1024]{2,0,1:T(8,128)S(1)}) fusion(f32[64,16,1024]{2,1,0:T(8,128)} %param.2, f32[64,16,1024]{2,0,1:T(8,128)} %copy-done.1, f32[64,1,1024]{2,0,1:T(8,128)S(1)} %collective-permute-done.1, ...), kind=kOutput, calls=%fused_computation.12 | output fusion | flops 76349440 | bytes 13893632 | tf_op jit(solution)/shard_map/jit(cumsum)/reduce_window_sum | solution.py:29
  36.6 0.1 pad_maximum_fusion.2
  36.7 0.7 copy.7
  37.4 2.5 %broadcast_in_dim.24 = f32[192,4,1024]{2,1,0:T(4,128)} broadcast(f32[]{:T(128)} %constant.24.clone.1), dimensions={} | broadcast | bytes 3145732 | tf_op jit(solution)/shard_map/broadcast_in_dim | solution.py:53
  39.8 8.1 %scatter_fusion = f32[192,4,1024]{2,1,0:T(4,128)} fusion(f32[192,4,1024]{2,1,0:T(4,128)} %broadcast_in_dim.24, s32[64]{0:T(128)S(1)} %compare_select_fusion.2, f32[64,4,1024]{2,1,0:T(4,128)S(1)} %copy.7), kind=kCustom, calls=%fused_computation.1 | custom fusion | bytes 3145984 | tf_op jit(solution)/shard_map/scatter | solution.py:53
  48.0 0.0 all-to-all-done
  48.0 4.2 %all-to-all-start.1 = ((f32[8,24,4,1024]{3,2,1,0:T(4,128)}), f32[8,24,4,1024]{3,2,1,0:T(4,128)S(1)}, u32[]{:S(2)}, u32[]{:S(2)}) async-start(f32[8,24,4,1024]{3,2,1,0:T(4,128)} %bitcast.4), calls=%async_computation.1 | async-start | bytes 6291456 | tf_op jit(solution)/shard_map/all_to_all | solution.py:95
  52.2 0.1 select_n.44
  52.3 37.7 %all-to-all-done.1 = f32[8,24,4,1024]{3,2,1,0:T(4,128)S(1)} async-done(((f32[8,24,4,1024]{3,2,1,0:T(4,128)}), f32[8,24,4,1024]{3,2,1,0:T(4,128)S(1)}, u32[]{:S(2)}, u32[]{:S(2)}) %all-to-all-start.1) | async-done | bytes 3145760 | tf_op jit(solution)/shard_map/all_to_all | solution.py:95
  90.0 0.0 copy-start
  90.0 1.7 %copy-done = f32[8,24,4,1024]{3,2,1,0:T(4,128)} copy-done((f32[8,24,4,1024]{3,2,1,0:T(4,128)}, f32[8,24,4,1024]{3,2,1,0:T(4,128)S(1)}, u32[]{:S(2)}) %copy-start) | copy-done | bytes 3145752
  91.7 0.2 broadcast_in_dim.20
  91.9 17.7 %scatter_fusion.1 = f32[65,4,1024]{2,1,0:T(4,128)S(1)} fusion(f32[65,4,1024]{2,1,0:T(4,128)S(1)} %broadcast_in_dim.20, s32[192]{0:T(256)S(1)} %bitcast.34, f32[192,4,1024]{2,1,0:T(4,128)} %bitcast.27), kind=kCustom, calls=%fused_computation.2 | custom fusion | bytes 9437952 | tf_op jit(solution)/shard_map/scatter | solution.py:69
  109.7 0.1 slice_bitcast_fusion
  109.7 27.7 %all_to_all.26 = f32[1,64,4,1024]{3,2,0,1:T(4,128)S(1)} all-to-all(f32[1,64,4,1024]{3,2,0,1:T(4,128)S(1)} %slice_bitcast_fusion), channel_id=1, replica_groups=mesh['depth'=4,'tile'=8] {'depth'}, dimensions={1} | all-to-all | bytes 2097152 | tf_op jit(solution)/shard_map/all_to_all | solution.py:80
  137.6 0.3 fusion.9
  137.9 0.2 fusion.5
  138.2 0.8 maximum_bitcast_fusion
  (11 shorter events, 0.2 us)
Async XLA Ops:
  0.0 13.8 %copy-start.2 = (s32[64]{0:T(128)S(1)}, s32[64]{0:T(128)}, u32[]{:S(2)}) copy-start(s32[64]{0:T(128)} %param.3) | copy-start | bytes 772
  4.9 1.9 %copy-start.1 = (f32[64,16,1024]{2,0,1:T(8,128)}, f32[64,16,1024]{2,0,1:T(8,128)S(1)}, u32[]{:S(2)}) copy-start(f32[64,16,1024]{2,0,1:T(8,128)S(1)} %copy_log_fusion) | copy-start | bytes 12582916
  6.9 12.9 %collective-permute-start = (f32[64,1,1024]{2,0,1:T(8,128)S(1)}, f32[64,1,1024]{2,0,1:T(8,128)S(1)}, u32[]{:S(2)}, u32[]{:S(2)}) collective-permute-start(f32[64,1,1024]{2,0,1:T(8,128)S(1)} %get-tuple-element.11), channel_id=1, source_target_pairs={{8,0},{16,8},{24,16},{9,1},{17,9},{25,17},{10,2},{18,10},{26,18},{... | collective-permute-start | bytes 786440 | tf_op jit(solution)/shard_map/ppermute | solution.py:15
  8.2 11.6 %collective-permute-start.1 = (f32[64,1,1024]{2,0,1:T(8,128)S(1)}, f32[64,1,1024]{2,0,1:T(8,128)S(1)}, u32[]{:S(2)}, u32[]{:S(2)}) collective-permute-start(f32[64,1,1024]{2,0,1:T(8,128)S(1)} %get-tuple-element.12), channel_id=1, source_target_pairs={{0,8},{8,16},{16,24},{1,9},{9,17},{17,25},{2,10},{10,18},{18,26},{... | collective-permute-start | bytes 786440 | tf_op jit(solution)/shard_map/ppermute | solution.py:12
  15.6 32.3 %all-to-all-start = ((f32[8,1,24]{2,1,0:T(1,128)}), f32[8,1,24]{2,1,0:T(1,128)S(1)}, u32[]{:S(2)}, u32[]{:S(2)}) async-start(f32[8,1,24]{2,1,0:T(1,128)} %all_to_all.18), calls=%async_computation | async-start | bytes 8192 | tf_op jit(solution)/shard_map/all_to_all | solution.py:96
  48.0 42.1 %all-to-all-start.1 = ((f32[8,24,4,1024]{3,2,1,0:T(4,128)}), f32[8,24,4,1024]{3,2,1,0:T(4,128)S(1)}, u32[]{:S(2)}, u32[]{:S(2)}) async-start(f32[8,24,4,1024]{3,2,1,0:T(4,128)} %bitcast.4), calls=%async_computation.1 | async-start | bytes 6291456 | tf_op jit(solution)/shard_map/all_to_all | solution.py:95
  90.0 1.7 %copy-start = (f32[8,24,4,1024]{3,2,1,0:T(4,128)}, f32[8,24,4,1024]{3,2,1,0:T(4,128)S(1)}, u32[]{:S(2)}) copy-start(f32[8,24,4,1024]{3,2,1,0:T(4,128)S(1)} %all-to-all-done.1) | copy-start | bytes 9437188
where the time goes:
time: 140 us; the launch traced here: 139 us
  local copies, waits for them, and re-layouts  39.5 us (28%)
  waiting for transfers between devices  37.7 us (27%)
  blocking collectives  27.7 us (20%)
  other arithmetic  18.6 us (13%)
  starting transfers between devices  15.3 us (11%)
    all_to_all x1, waiting for transfers between devices, local(): lax.all_to_all(buffer, 'tile', split_axis=0, concat_axis=0, tiled=True)  37.7 us
    all_to_all x1, blocking collectives, merge_depth(): lax.all_to_all(layers.reshape((1,) + layers.shape), 'depth', split_axis=1...  27.7 us
    scatter x1, local copies, waits for them, and re-layouts, place(): jnp.zeros((count + 1,) + flat.shape[1:], jnp.float32).at[target].set(flat)  17.7 us
    another operation x1, other arithmetic, shade_rays(): depth_sum = jnp.cumsum(optical, axis=1)  16.7 us
    scatter x1, local copies, waits for them, and re-layouts, pack_groups(): jnp.zeros((groups * slots,) + values.shape[1:], jnp.float32).at[target]  8.13 us
    ppermute x1, starting transfers between devices, extended(): lax.ppermute(lax.slice_in_dim(block, block.shape[dim] - width, None, axis...  5.6 us
    log x1, local copies, waits for them, and re-layouts, slab_layers(): level = jnp.log(density)  4.9 us
    all_to_all x1, starting transfers between devices, local(): lax.all_to_all(buffer, 'tile', split_axis=0, concat_axis=0, tiled=True)  4.21 us
  transfers between devices with their start and end apart: 4, of which 1 were waited for; matrix products, arithmetic and copies ran while one was open for 21% of the time, Pallas kernels for 0%

commit v1 on v0

v1 whole, which is shorter than its diff:
```python
import functools
import math

import jax
import jax.numpy as jnp
from jax import lax
from jax.experimental import pallas as pl
from jax.experimental.pallas import tpu as pltpu
from jax.sharding import PartitionSpec as P

LANES = 128
ROWS = 8
GROUP = 16
HIGHEST = lax.Precision.HIGHEST


def render_kernel(
    depths, tiles, per, cells, pix, cap, pad,
    patches, slot, out,
    grid, low, high, lay, got, packed, labels, recv, marks, final, back,
    load_sem, halo_send, halo_recv, lay_send, lay_recv, tile_send, tile_recv, mark_send, mark_recv,
    back_send, back_recv,
):
    z = lax.axis_index("depth")
    me = lax.axis_index("tile")
    wide = depths * LANES
    chunks = pix // wide
    groups = per // GROUP
    share = per // depths
    scale = 2.0 / (cells * depths)

    def other(delta):
        return lax.rem(z + delta, depths)

    def peer(delta):
        return lax.rem(me + delta, tiles)

    def load(c, k):
        lanes = pl.ds(c * wide, wide)
        return pltpu.make_async_copy(patches.at[:, k, lanes], grid.at[k, c], load_sem.at[c, k])

    def halo_up(c, g):
        rows = pl.ds(pl.multiple_of(g * GROUP, GROUP), GROUP)
        return pltpu.make_async_remote_copy(
            grid.at[cells - 1, c, rows], low.at[c, rows], halo_send.at[0, c, g], halo_recv.at[0, c, g],
            device_id={"depth": z + 1}, device_id_type=pl.DeviceIdType.MESH)

    def halo_down(c, g):
        rows = pl.ds(pl.multiple_of(g * GROUP, GROUP), GROUP)
        return pltpu.make_async_remote_copy(
            grid.at[0, c, rows], high.at[c, rows], halo_send.at[1, c, g], halo_recv.at[1, c, g],
            device_id={"depth": z - 1}, device_id_type=pl.DeviceIdType.MESH)

    def send_lay(c, g, delta):
        rows = pl.ds(pl.multiple_of(g * GROUP, GROUP), GROUP)
        to = other(delta)
        return pltpu.make_async_remote_copy(
            lay.at[c, to, rows], got.at[c, z, rows], lay_send.at[c, g, to], lay_recv.at[c, g, z],
            device_id={"depth": to}, device_id_type=pl.DeviceIdType.MESH)

    def take_lay(c, g, delta):
        rows = pl.ds(pl.multiple_of(g * GROUP, GROUP), GROUP)
        src = other(delta)
        return pltpu.make_async_remote_copy(
            lay.at[c, src, rows], got.at[c, src, rows], lay_send.at[c, g, src], lay_recv.at[c, g, src],
            device_id={"depth": src}, device_id_type=pl.DeviceIdType.MESH)

    def send_tile(c, delta):
        to = peer(delta)
        return pltpu.make_async_remote_copy(
            packed.at[c, to], recv.at[c, me], tile_send.at[c, to], tile_recv.at[c, me],
            device_id={"tile": to}, device_id_type=pl.DeviceIdType.MESH)

    def take_tile(c, src):
        return pltpu.make_async_remote_copy(
            packed.at[c, src], recv.at[c, src], tile_send.at[c, src], tile_recv.at[c, src],
            device_id={"tile": src}, device_id_type=pl.DeviceIdType.MESH)

    def send_mark(delta):
        to = peer(delta)
        return pltpu.make_async_remote_copy(
            labels.at[to], marks.at[me], mark_send.at[to], mark_recv.at[me],
            device_id={"tile": to}, device_id_type=pl.DeviceIdType.MESH)

    def take_mark(src):
        return pltpu.make_async_remote_copy(
            labels.at[src], marks.at[src], mark_send.at[src], mark_recv.at[src],
            device_id={"tile": src}, device_id_type=pl.DeviceIdType.MESH)

    def send_back(c, delta):
        to = other(delta)
        return pltpu.make_async_remote_copy(
            final.at[c, to], back.at[c, z], back_send.at[c, to], back_recv.at[c, z],
            device_id={"depth": to}, device_id_type=pl.DeviceIdType.MESH)

    def take_back(c, delta):
        src = other(delta)
        return pltpu.make_async_remote_copy(
            final.at[c, src], back.at[c, src], back_send.at[c, src], back_recv.at[c, src],
            device_id={"depth": src}, device_id_type=pl.DeviceIdType.MESH)

    order = [0, cells - 1] + list(range(1, cells - 1))
    for c in range(chunks):
        for k in order[:2]:
            load(c, k).start()
    for c in range(chunks):
        for k in order[2:]:
            load(c, k).start()

    barrier = pltpu.get_barrier_semaphore()
    for delta in range(1, depths):
        pl.semaphore_signal(barrier, inc=1, device_id={"depth": other(delta)}, device_id_type=pl.DeviceIdType.MESH)

    @pl.loop(1, tiles)
    def _(delta):
        pl.semaphore_signal(barrier, inc=1, device_id={"tile": peer(delta)}, device_id_type=pl.DeviceIdType.MESH)

    @pl.when(z == 0)
    def _():
        low[...] = jnp.ones_like(low)

    @pl.when(z == depths - 1)
    def _():
        high[...] = jnp.ones_like(high)

    bits = int(math.log2(per))
    line = lax.broadcasted_iota(jnp.int32, (per, per), 0)
    column = lax.broadcasted_iota(jnp.int32, (per, per), 1)
    slot_row = jnp.broadcast_to(slot[...], (per, per))
    slot_col = jnp.broadcast_to(
        jnp.sum(jnp.where(line == column, slot_row, 0), axis=1, keepdims=True), (per, per))
    owner_row = lax.shift_right_logical(slot_row, bits)
    owner_col = lax.shift_right_logical(slot_col, bits)
    same = owner_row == owner_col
    rank_row = jnp.sum(jnp.where(same & (line < column), 1, 0), axis=0, keepdims=True)
    rank_col = jnp.sum(jnp.where(same & (column < line), 1, 0), axis=1, keepdims=True)
    target = owner_row[:1] * pad + rank_row
    place = lax.broadcasted_iota(jnp.int32, (tiles * pad, per), 0)
    spread = (place == jnp.broadcast_to(target, (tiles * pad, per))).astype(jnp.float32)
    offset = (slot_col[:, :1] & (per - 1)) + 1
    spot = lax.broadcasted_iota(jnp.int32, (per, LANES), 1)
    tagged = jnp.where(spot == jnp.broadcast_to(rank_col, (per, LANES)),
                       jnp.broadcast_to(offset, (per, LANES)), 0).astype(jnp.float32)
    holder = lax.shift_right_logical(lax.broadcasted_iota(jnp.int32, (tiles * ROWS, per), 0), 3)
    mine = (holder == jnp.broadcast_to(owner_row[:1], (tiles * ROWS, per))).astype(jnp.float32)
    named = jnp.dot(mine, tagged, precision=HIGHEST, preferred_element_type=jnp.float32) - 1.0
    labels[...] = named.reshape(tiles, ROWS, LANES)

    pl.semaphore_wait(barrier, depths + tiles - 2)

    for c in range(chunks):
        for k in order[:2]:
            load(c, k).wait()
        for g in range(groups):
            @pl.when(z < depths - 1)
            def _():
                halo_up(c, g).start()

            @pl.when(z > 0)
            def _():
                halo_down(c, g).start()

    @pl.loop(1, tiles)
    def _(delta):
        send_mark(delta).start()

    marks[me] = labels[me]

    for c in range(chunks):
        for k in order[2:]:
            load(c, k).wait()

        @pl.loop(0, groups)
        def _(g):
            @pl.when(z > 0)
            def _():
                halo_up(c, g).wait_recv()

            @pl.when(z < depths - 1)
            def _():
                halo_down(c, g).wait_recv()

            @pl.loop(0, GROUP // ROWS)
            def _(half):
                rows = pl.ds(pl.multiple_of(g * GROUP + half * ROWS, ROWS), ROWS)
                before = jnp.log(low[c, rows])
                density = grid[0, c, rows]
                level = jnp.log(density)
                remain = red = green = blue = None
                for k in range(cells):
                    later = grid[k + 1, c, rows] if k + 1 < cells else high[c, rows]
                    after = jnp.log(later)
                    slope = (after - before) * 0.5
                    steep = slope * slope
                    bell = jnp.exp(-(level * level))
                    square = density * density
                    dim = 1.0 + steep
                    both = dim * (1.0 + square)
                    inverse = 1.0 / (both * square)
                    tail = bell * (inverse * both)
                    tau = (
                        (0.6 * math.exp(-0.25) * scale) * (bell * density)
                        + (0.4 * math.exp(-2.0) * scale) * (tail * tail)
                        + (0.3 * scale) * steep
                    )
                    pass_on = jnp.exp(-tau)
                    lost = 1.0 - pass_on
                    weight = lost if remain is None else remain * lost
                    lit = weight * (inverse * square)
                    r, gr, b = lit * square, lit * (1.0 + square) * bell, lit
                    if remain is None:
                        remain, red, green, blue = pass_on, r, gr, b
                    else:
                        remain, red, green, blue = remain * pass_on, red + r, green + gr, blue + b
                    before, level, density = level, after, later
                for j in range(depths):
                    for ch, value in enumerate((red, green, blue, remain)):
                        lay[c, j, rows, ch * LANES:(ch + 1) * LANES] = value[:, j * LANES:(j + 1) * LANES]

            for delta in range(1, depths):
                send_lay(c, g, delta).start()

    for c in range(chunks):
        got[c, z] = lay[c, z]

        @pl.loop(0, groups)
        def _(g):
            for delta in range(1, depths):
                take_lay(c, g, delta).wait_recv()

        red = [got[c, 0, :, ch * LANES:(ch + 1) * LANES] for ch in range(4)]
        for s in range(1, depths):
            for ch in range(3):
                red[ch] = red[ch] + red[3] * got[c, s, :, ch * LANES:(ch + 1) * LANES]
            red[3] = red[3] * got[c, s, :, 3 * LANES:]
        red[3] = 1.0 - red[3]
        for ch in range(4):
            block = jnp.dot(spread, red[ch], precision=HIGHEST, preferred_element_type=jnp.float32)
            packed[c, :, :, ch * LANES:(ch + 1) * LANES] = block.reshape(tiles, pad, LANES)

        @pl.loop(1, tiles)
        def _(delta):
            send_tile(c, delta).start()

        recv[c, me] = packed[c, me]

    number = lax.broadcasted_iota(jnp.int32, (per, pad), 0).astype(jnp.float32)
    for c in range(chunks):
        if c == 0:
            @pl.loop(1, tiles)
            def _(delta):
                take_mark(peer(delta)).wait_recv()

        @pl.loop(1, tiles)
        def _(delta):
            take_tile(c, peer(delta)).wait_recv()

        total = jnp.zeros((per, 4 * LANES), jnp.float32)
        for s in range(tiles):
            pick = (number == jnp.broadcast_to(marks[s, 0:1, 0:pad], (per, pad))).astype(jnp.float32)
            total = total + jnp.dot(pick, recv[c, s], precision=HIGHEST, preferred_element_type=jnp.float32)
        final[c] = total.reshape(depths, share, 4 * LANES)
        for delta in range(1, depths):
            send_back(c, delta).start()
        back[c, z] = final[c, z]

    for c in range(chunks):
        for delta in range(1, depths):
            take_back(c, delta).wait_recv()
        for s in range(depths):
            for ch in range(4):
                start = ch * pix + c * wide + s * LANES
                out[:, start:start + LANES] = back[c, s, :, ch * LANES:(ch + 1) * LANES]

    for c in range(chunks):
        for g in range(groups):
            @pl.when(z < depths - 1)
            def _():
                halo_up(c, g).wait_send()

            @pl.when(z > 0)
            def _():
                halo_down(c, g).wait_send()

            for delta in range(1, depths):
                send_lay(c, g, delta).wait_send()

        @pl.loop(1, tiles)
        def _(delta):
            send_tile(c, delta).wait_send()

        for delta in range(1, depths):
            send_back(c, delta).wait_send()

    @pl.loop(1, tiles)
    def _(delta):
        send_mark(delta).wait_send()


def local(patches, patch_slot):
    per, cells, pix = patches.shape
    depths, tiles = lax.axis_size("depth"), lax.axis_size("tile")
    cap = 3 * per // tiles
    pad = -(-cap // ROWS) * ROWS
    wide = depths * LANES
    chunks, groups, share = pix // wide, per // GROUP, per // depths
    row = 4 * LANES
    f32 = jnp.float32
    dma = pltpu.SemaphoreType.DMA
    image = pl.pallas_call(
        functools.partial(render_kernel, depths, tiles, per, cells, pix, cap, pad),
        out_shape=jax.ShapeDtypeStruct((share, 4 * pix), f32),
        in_specs=[pl.BlockSpec(memory_space=pl.ANY), pl.BlockSpec(memory_space=pltpu.VMEM)],
        out_specs=pl.BlockSpec(memory_space=pltpu.VMEM),
        scratch_shapes=[
            pltpu.VMEM((cells, chunks, per, wide), f32),
            pltpu.VMEM((chunks, per, wide), f32),
            pltpu.VMEM((chunks, per, wide), f32),
            pltpu.VMEM((chunks, depths, per, row), f32),
            pltpu.VMEM((chunks, depths, per, row), f32),
            pltpu.VMEM((chunks, tiles, pad, row), f32),
            pltpu.VMEM((tiles, ROWS, LANES), f32),
            pltpu.VMEM((chunks, tiles, pad, row), f32),
            pltpu.VMEM((tiles, ROWS, LANES), f32),
            pltpu.VMEM((chunks, depths, share, row), f32),
            pltpu.VMEM((chunks, depths, share, row), f32),
            dma((chunks, cells)),
            dma((2, chunks, groups)), dma((2, chunks, groups)),
            dma((chunks, groups, depths)), dma((chunks, groups, depths)),
            dma((chunks, tiles)), dma((chunks, tiles)),
            dma((tiles,)), dma((tiles,)),
            dma((chunks, depths)), dma((chunks, depths)),
        ],
        compiler_params=pltpu.CompilerParams(
            collective_id=0, has_side_effects=True, vmem_limit_bytes=48 * 1024 * 1024),
        name="render",
    )(patches, patch_slot.reshape(1, per))
    return image.reshape(1, share, 4, pix)


def solution(mesh):
    return jax.shard_map(
        local,
        mesh=mesh,
        in_specs=(P("tile", "depth", None), P("tile")),
        out_specs=P("tile", "depth", None, None),
        check_vma=False,
    )
```

time: 140 us -> 54 us (0.39)
  Pallas kernels: 0 us -> 50.1 us
  waiting for transfers between devices: 37.7 us -> 0 us
  local copies, waits for them, and re-layouts: 39.5 us -> 3.72 us
  blocking collectives: 27.7 us -> 0 us
  other arithmetic: 18.6 us -> 0 us
  starting transfers between devices: 15.3 us -> 0 us
    pallas_call x0 -> x1, Pallas kernels: none -> 50.1 us  [local(): pl.pallas_call(functools.partial(render_kernel, depths, tiles, per, cells...]
    all_to_all x2 -> x0, waiting for transfers between devices: 37.7 us -> none  [the longest x1 37.7 us: local(): lax.all_to_all(buffer, 'tile', split_axis=0, concat_axis=0, tiled=True)]
    all_to_all x1 -> x0, blocking collectives: 27.7 us -> none  [merge_depth(): lax.all_to_all(layers.reshape((1,) + layers.shape), 'depth', split_axis=1...]
    scatter x3 -> x0, local copies, waits for them, and re-layouts: 26.6 us -> none  [the longest x1 17.7 us: place(): jnp.zeros((count + 1,) + flat.shape[1:], jnp.float32).at[target].set(flat)]
    another operation x3 -> x0, other arithmetic: 16.9 us -> none  [the longest x1 16.7 us: shade_rays(): depth_sum = jnp.cumsum(optical, axis=1)]
    all_to_all x2 -> x0, starting transfers between devices: 8.37 us -> none  [the longest x1 4.21 us: local(): lax.all_to_all(buffer, 'tile', split_axis=0, concat_axis=0, tiled=True)]
    ppermute x2 -> x0, starting transfers between devices: 6.89 us -> none  [the longest x1 5.6 us: extended(): lax.ppermute(lax.slice_in_dim(block, block.shape[dim] - width, None, axis...]
    log x1 -> x0, local copies, waits for them, and re-layouts: 4.9 us -> none  [slab_layers(): level = jnp.log(density)]
  transfers between devices with their start and end apart: 4 -> 0, of which waited for: 1 -> 0; matrix products, arithmetic and copies ran while one was open for 21% -> 0% of each run, Pallas kernels for 0% -> 0%
where the time goes in v1:
time: 54 us; the launch traced here: 53.9 us
  Pallas kernels  50.1 us (93%)
  local copies, waits for them, and re-layouts  3.72 us (7%)
    pallas_call x1, Pallas kernels, local(): pl.pallas_call(functools.partial(render_kernel, depths, tiles, per, cells...  50.1 us
    unnamed x4, local copies, waits for them, and re-layouts  2.84 us

profile of v1, /device:TPU:0, one launch (start us, length us, event | category | flops | bytes accessed | tf_op | source)
XLA Modules:
  0.0 53.9 jit_solution(18003837219460299677)
XLA Ops:
  0.0 0.0 copy-start
  0.0 2.2 %copy-done = f32[64,16,1024]{2,1,0:T(8,128)S(1)} copy-done((f32[64,16,1024]{2,1,0:T(8,128)S(1)}, f32[64,16,1024]{2,1,0:T(8,128)}, u32[]{:S(2)}) %copy-start) | copy-done | bytes 4194328
  2.2 0.0 copy-start.1
  2.2 0.7 %copy-done.1 = s32[64]{0:T(128)S(1)} copy-done((s32[64]{0:T(128)S(1)}, s32[64]{0:T(128)}, u32[]{:S(2)}) %copy-start.1) | copy-done | bytes 280
  2.8 50.1 %render.1 = f32[16,4096]{1,0:T(8,128)S(1)} custom-call(f32[64,16,1024]{2,1,0:T(8,128)S(1)} %copy-done, s32[1,64]{1,0:T(1,128)S(1)} %bitcast.1), custom_call_target="tpu_custom_call" | custom-call | tf_op jit(solution)/shard_map/render/pallas_call | solution.py:310
  53.0 0.9 %reshape.7 = f32[1,16,4,1024]{3,2,1,0:T(4,128)} reshape(f32[16,4096]{1,0:T(8,128)S(1)} %render.1) | data formatting | bytes 524288 | tf_op jit(solution)/shard_map/reshape | solution.py:338
Async XLA Ops:
  0.0 2.2 %copy-start = (f32[64,16,1024]{2,1,0:T(8,128)S(1)}, f32[64,16,1024]{2,1,0:T(8,128)}, u32[]{:S(2)}) copy-start(f32[64,16,1024]{2,1,0:T(8,128)} %patches.1) | copy-start | bytes 12582916
  2.2 0.7 %copy-start.1 = (s32[64]{0:T(128)S(1)}, s32[64]{0:T(128)}, u32[]{:S(2)}) copy-start(s32[64]{0:T(128)} %param.3) | copy-start | bytes 772
